TPU v7x, 32 devices: a whole 2x2x4 slice. The times are simulated.
32 devices in a mesh: prow: 4 (over y, x), pcol: 8 (over z, core).
Axes of the slice: x: 2, y: 2, z: 4, core: 2. Of those that a mesh axis runs over, the one named last changes fastest.
Arguments:
- anc_inverse: bfloat16 [6, 1024, 3, 2048], P(None, 'prow', None, 'pcol'), may hold values from -0.078125 to 0.078125
- panel: bfloat16 [3, 6, 4, 256, 512], P(None, None, 'prow', 'pcol'), may hold values from -1.1953125 to 1.1953125
- tile_mask: int32 [3, 24], replicated, may hold values 0 or 1
- diag_inverse: float32 [3, 512, 512], P(None, ('prow', 'pcol')), may hold values from -6 to 6
Outputs:
- block_column: bfloat16 [3, 6, 4, 256, 512], P(None, None, 'prow', 'pcol')
- diag_block: float32 [3, 512, 512], P(None, ('prow', 'pcol'))
All inputs are finite; a program needn't handle non-finite values.
Results may differ from a plain program's by a relative error of at most 0.0017.
Values may be sent and summed in bfloat16 or wider, within the bound.
No kernel may reach another device: no remote copies, remote signals or barrier semaphores. Data moves between devices by JAX's collectives and lax.ppermute only.
A program may use at most 128 MiB of HBM per device.

v0:
```python
import jax
import jax.numpy as jnp
from jax import lax
from jax.sharding import PartitionSpec as P


def spread(x, axis, root):
    mine = lax.axis_index(axis) == root
    return lax.psum(jnp.where(mine, x, jnp.zeros_like(x)), axis)


def local_product(anc_block, columns):
    return jnp.einsum("aibj,sbjw->isaw", anc_block, columns, preferred_element_type=jnp.float32)


def outbound(masked, n_row, n_col):
    groups, tile_rows, single, sub_rows, width = masked.shape
    tile_cols = tile_rows * n_row // n_col
    grouped = masked.reshape(groups, tile_cols, n_col // n_row, sub_rows, width)
    return jnp.repeat(grouped, n_row, axis=2)


def body(anc_inverse, panel, tile_mask, diag_inverse):
    n_row = lax.axis_size("prow")
    n_col = lax.axis_size("pcol")
    row_pos = lax.axis_index("prow")
    col_pos = lax.axis_index("pcol")
    sets, tile_rows, single, sub_rows, width = panel.shape
    tiles = tile_mask.shape[1]
    tile_size = anc_inverse.shape[1]
    row_ids = jnp.arange(tile_rows, dtype=jnp.int32) * n_row + row_pos
    hits = (row_ids[:, None] == jnp.arange(tiles, dtype=jnp.int32)[None, :]).astype(jnp.int32)
    row_mask = jnp.sum(tile_mask[:, None, :] * hits[None], axis=2)
    keep = row_mask.astype(jnp.bfloat16)[:, :, None, None, None]
    masked = panel * keep
    outgoing = outbound(masked, n_row, n_col)
    root = col_pos % n_row
    arrived = lax.all_to_all(outgoing, "pcol", split_axis=2, concat_axis=3, tiled=True)
    columns = spread(arrived.reshape(sets, -1, tile_size, width), "prow", root)
    summed = lax.psum_scatter(
        local_product(anc_inverse, columns), "pcol", scatter_dimension=0, tiled=True
    )
    image = -jnp.transpose(summed, (1, 2, 0, 3))[:, :, None] * keep.astype(jnp.float32)
    block_column = image.astype(jnp.bfloat16)
    partial_value = jnp.einsum(
        "saxiw,saxiv->swv", masked, block_column, preferred_element_type=jnp.float32
    )
    mine = lax.psum_scatter(partial_value, ("prow", "pcol"), scatter_dimension=1, tiled=True)
    diag_block = diag_inverse - mine
    return (block_column, diag_block)


def solution(mesh):
    in_specs = (
        P(None, "prow", None, "pcol"),
        P(None, None, "prow", "pcol", None),
        P(),
        P(None, ("prow", "pcol"), None),
    )
    out_specs = (P(None, None, "prow", "pcol", None), P(None, ("prow", "pcol"), None))
    return jax.shard_map(body, mesh=mesh, in_specs=in_specs, out_specs=out_specs, check_vma=False)
```

profile of v0, /device:TPU:0, one launch (start us, length us, event | category | flops | bytes accessed | tf_op | source)
XLA Modules:
  0.0 455.2 jit_solution(3141937686562053441)
XLA Ops:
  7.2 0.0 copy-start
  7.2 0.1 fusion.6
  7.3 1.0 multiply_reduce_fusion
  8.2 1.2 broadcast_multiply_fusion
  9.4 0.0 copy-start.1
  9.4 0.8 copy-done.1
  10.3 1.7 broadcast_in_dim.4
  12.0 6.4 %all-to-all-start = ((bf16[3,3,8,32,512]{4,3,1,0,2:T(8,128)(2,1)}), bf16[3,3,8,32,512]{4,3,1,0,2:T(8,128)(2,1)}, u32[]{:S(2)}, u32[]{:S(2)}) async-start(bf16[3,3,8,32,512]{4,3,1,0,2:T(8,128)(2,1)} %bitcast.27), calls=%async_computation | async-start | bytes 4718592 | tf_op jit(solution)/shard_map/all_to_all | solution.py:38
  18.4 0.0 all-reduce.2.cloned.1.call-start
  18.4 54.7 %all-to-all-done = bf16[3,3,8,32,512]{4,3,1,0,2:T(8,128)(2,1)} async-done(((bf16[3,3,8,32,512]{4,3,1,0,2:T(8,128)(2,1)}), bf16[3,3,8,32,512]{4,3,1,0,2:T(8,128)(2,1)}, u32[]{:S(2)}, u32[]{:S(2)}) %all-to-all-start) | async-done | bytes 2359328 | tf_op jit(solution)/shard_map/all_to_all | solution.py:38
  73.1 3.2 copy_select_fusion
  76.3 4.3 copy.20
  80.6 0.0 all-reduce.2.cloned.1.call-update
  80.6 0.0 reduce-scatter.3.cloned.1.call-start
  80.7 72.9 %all-reduce.2.cloned.1.call-done = bf16[3,3,256,512]{2,3,1,0:T(8,128)(2,1)} async-done(((bf16[3,3,256,512]{2,3,1,0:T(8,128)(2,1)}), bf16[3,3,256,512]{2,3,1,0:T(8,128)(2,1)}) %all-reduce.2.cloned.1.call-update) | async-done | bytes 2359312 | tf_op jit(solution)/shard_map/psum | solution.py:9
  153.6 0.0 copy-done
  153.6 7.9 %convolution_bitcast_fusion = f32[256,3,6,512]{0,3,2,1:T(8,128)} fusion(bf16[3,3,256,512]{2,3,1,0:T(8,128)(2,1)} %all-reduce.2.cloned.1.call-done, bf16[6,256,3,256]{3,1,2,0:T(8,128)(2,1)S(1)} %copy-done), kind=kOutput, calls=%fused_computation | convolution fusion | flops 3623878656 | bytes 14155776 | tf_op jit(solution)/shard_map/aibj,sbjw->isaw/dot_general | solution.py:13
  161.5 11.9 %copy.21 = f32[256,3,6,512]{3,2,1,0:T(8,128)} copy(f32[256,3,6,512]{0,3,2,1:T(8,128)} %convolution_bitcast_fusion) | data formatting | bytes 18874368 | tf_op jit(solution)/shard_map/aibj,sbjw->isaw/transpose | solution.py:13
  173.4 0.0 reduce-scatter.3.cloned.1.call-update
  173.4 0.0 reduce-scatter.5.cloned.1.call-start
  173.4 129.2 %reduce-scatter.3.cloned.1.call-done = f32[32,3,6,512]{3,2,1,0:T(8,128)} async-done(((f32[256,3,6,512]{3,2,1,0:T(8,128)}), f32[32,3,6,512]{3,2,1,0:T(8,128)}) %reduce-scatter.3.cloned.1.call-update) | async-done | bytes 1179664 | tf_op jit(solution)/shard_map/reduce_scatter | solution.py:40
  302.7 1.8 fusion.5
  304.4 3.4 convolution_bitcast_fusion.1
  307.8 0.0 copy-start.2
  307.8 0.0 reduce-scatter.5.cloned.1.call-update
  307.8 1.0 copy.23
  308.8 138.3 %reduce-scatter.5.cloned.1.call-done = f32[3,16,512]{2,1,0:T(8,128)} async-done(((f32[3,512,512]{2,1,0:T(8,128)}), f32[3,16,512]{2,1,0:T(8,128)}) %reduce-scatter.5.cloned.1.call-update) | async-done | bytes 98320 | tf_op jit(solution)/shard_map/reduce_scatter | solution.py:48
  447.1 0.0 copy-done.2
  447.1 1.5 sub.3
  (3 shorter events, 0.1 us)
Async XLA Ops:
  7.2 146.4 %copy-start = (bf16[6,256,3,256]{3,1,2,0:T(8,128)(2,1)S(1)}, bf16[6,256,3,256]{3,1,2,0:T(8,128)(2,1)}, u32[]{:S(2)}) copy-start(bf16[6,256,3,256]{3,1,2,0:T(8,128)(2,1)} %param.4) | copy-start | bytes 7077892
  9.4 0.8 copy-start.1
  12.0 61.1 %all-to-all-start = ((bf16[3,3,8,32,512]{4,3,1,0,2:T(8,128)(2,1)}), bf16[3,3,8,32,512]{4,3,1,0,2:T(8,128)(2,1)}, u32[]{:S(2)}, u32[]{:S(2)}) async-start(bf16[3,3,8,32,512]{4,3,1,0,2:T(8,128)(2,1)} %bitcast.27), calls=%async_computation | async-start | bytes 4718592 | tf_op jit(solution)/shard_map/all_to_all | solution.py:38
  18.4 135.2 %all-reduce.2.cloned.1.call-start = ((), (), s32[]{:S(2)}) async-start(), calls=%async_computation.3 | async-start | bytes 4718592 | tf_op jit(solution)/shard_map/psum | solution.py:9
  80.6 222.0 %reduce-scatter.3.cloned.1.call-start = ((), (), s32[]{:S(2)}) async-start(), calls=%async_computation.4 | async-start | bytes 14155776 | tf_op jit(solution)/shard_map/reduce_scatter | solution.py:40
  173.4 273.7 %reduce-scatter.5.cloned.1.call-start = ((), (), s32[]{:S(2)}) async-start(), calls=%async_computation.5 | async-start | bytes 3244032 | tf_op jit(solution)/shard_map/reduce_scatter | solution.py:48
  307.8 139.3 %copy-start.2 = (f32[3,16,512]{2,1,0:T(8,128)S(1)}, f32[3,16,512]{2,1,0:T(8,128)}, u32[]{:S(2)}) copy-start(f32[3,16,512]{2,1,0:T(8,128)} %param.7) | copy-start | bytes 294916
Sparse Core Ops, SparseCore 0:
  80.7 72.7 all-reduce.1
  173.5 129.1 reduce-scatter.2
  308.0 139.0 reduce-scatter.4
where the time goes:
time: 456 us; the launch traced here: 455 us
  waiting for transfers between devices  395 us (87%)
  local copies, waits for them, and re-layouts  19.7 us (4%)
  between operations  13.8 us (3%)
  matrix products  11.3 us (2%)
  other arithmetic  8.76 us (2%)
  starting transfers between devices  6.47 us (1%)
    reduce_scatter x1, waiting for transfers between devices, body(): lax.psum_scatter(partial_value, ('prow', 'pcol'), scatter_dimension=1, ti...  138 us
    reduce_scatter x1, waiting for transfers between devices, body(): lax.psum_scatter(local_product(anc_inverse, columns), 'pcol', scatter_dim...  129 us
    psum x1, waiting for transfers between devices, spread(): return lax.psum(jnp.where(mine, x, jnp.zeros_like(x)), axis)  72.9 us
    all_to_all x1, waiting for transfers between devices, body(): lax.all_to_all(outgoing, 'pcol', split_axis=2, concat_axis=3, tiled=True)  54.7 us
    transpose x1, local copies, waits for them, and re-layouts, local_product(): jnp.einsum('aibj,sbjw->isaw', anc_block, columns, preferred_element_type=...  11.9 us
  transfers between devices with their start and end apart: 4, of which 4 were waited for; matrix products, arithmetic and copies ran while one was open for 0% of the time, Pallas kernels for 0%

commit v1 on v0

--- a/solution.py
+++ b/solution.py
@@ -35,7 +35,10 @@
     masked = panel * keep
     outgoing = outbound(masked, n_row, n_col)
     root = col_pos % n_row
-    arrived = lax.all_to_all(outgoing, "pcol", split_axis=2, concat_axis=3, tiled=True)
+    arrived = jnp.concatenate(
+        lax.all_to_all(jnp.stack(jnp.split(outgoing, lax.axis_size("pcol"), axis=2)), "pcol", 0, 0),
+        axis=3,
+    )
     columns = spread(arrived.reshape(sets, -1, tile_size, width), "prow", root)
     summed = lax.psum_scatter(
         local_product(anc_inverse, columns), "pcol", scatter_dimension=0, tiled=True

time: 456 us -> 461 us (1.011)
  local copies, waits for them, and re-layouts: 19.7 us -> 25.8 us
    unnamed x7 -> x14, local copies, waits for them, and re-layouts: 1.82 us -> 7.03 us
where the time goes in v1:
time: 461 us; the launch traced here: 460 us
  waiting for transfers between devices  395 us (86%)
  local copies, waits for them, and re-layouts  25.8 us (6%)
  between operations  13.8 us (3%)
  matrix products  11.3 us (2%)
  other arithmetic  7.36 us (2%)
  starting transfers between devices  6.47 us (1%)
    reduce_scatter x1, waiting for transfers between devices, body(): lax.psum_scatter(partial_value, ('prow', 'pcol'), scatter_dimension=1, ti...  139 us
    reduce_scatter x1, waiting for transfers between devices, body(): lax.psum_scatter(local_product(anc_inverse, columns), 'pcol', scatter_dim...  129 us
    psum x1, waiting for transfers between devices, spread(): return lax.psum(jnp.where(mine, x, jnp.zeros_like(x)), axis)  72.6 us
    all_to_all x1, waiting for transfers between devices, body(): lax.all_to_all(jnp.stack(jnp.split(outgoing, lax.axis_size('pcol'), axis=...  54.7 us
    transpose x1, local copies, waits for them, and re-layouts, local_product(): jnp.einsum('aibj,sbjw->isaw', anc_block, columns, preferred_element_type=...  11.9 us
  transfers between devices with their start and end apart: 4, of which 4 were waited for; matrix products, arithmetic and copies ran while one was open for 0% of the time, Pallas kernels for 0%

profile of v1, /device:TPU:0, one launch (start us, length us, event | category | flops | bytes accessed | tf_op | source)
XLA Modules:
  0.0 460.2 jit_solution(8669992832942973123)
XLA Ops:
  7.2 0.0 copy-start
  7.2 0.1 fusion.14
  7.3 1.0 multiply_reduce_fusion
  8.2 1.2 broadcast_multiply_fusion
  9.4 0.0 copy-start.1
  9.4 0.8 copy-done.1
  10.3 0.3 broadcast_in_dim.4
  10.6 0.8 fusion.11
  11.3 0.7 fusion.10
  12.1 0.7 fusion.9
  12.8 0.7 fusion.8
  13.6 0.7 fusion.7
  14.3 0.8 fusion.6
  15.1 0.7 fusion.5
  15.8 0.8 fusion.4
  16.6 6.4 %all-to-all-start = ((bf16[8,3,3,1,32,512]{5,4,2,1,3,0:T(8,128)(2,1)}), bf16[8,3,3,1,32,512]{5,4,2,1,3,0:T(8,128)(2,1)}, u32[]{:S(2)}, u32[]{:S(2)}) async-start(bf16[8,3,3,1,32,512]{5,4,2,1,3,0:T(8,128)(2,1)} %fusion.4), calls=%async_computation | async-start | bytes 4718592 | tf_op jit(solution)/shard_map/all_to_all | solution.py:39
  22.9 0.0 all-reduce.2.cloned.1.call-start
  23.0 54.7 %all-to-all-done = bf16[8,3,3,1,32,512]{5,4,2,1,3,0:T(8,128)(2,1)} async-done(((bf16[8,3,3,1,32,512]{5,4,2,1,3,0:T(8,128)(2,1)}), bf16[8,3,3,1,32,512]{5,4,2,1,3,0:T(8,128)(2,1)}, u32[]{:S(2)}, u32[]{:S(2)}) %all-to-all-start) | async-done | bytes 2359328 | tf_op jit(solution)/shard_map/all_to_all | solution.py:39
  77.7 1.8 select_bitcast_fusion
  79.5 1.6 copy.28
  81.1 4.3 copy.29
  85.4 0.0 all-reduce.2.cloned.1.call-update
  85.4 0.0 reduce-scatter.3.cloned.1.call-start
  85.4 72.6 %all-reduce.2.cloned.1.call-done = bf16[3,3,256,512]{2,3,1,0:T(8,128)(2,1)} async-done(((bf16[3,3,256,512]{2,3,1,0:T(8,128)(2,1)}), bf16[3,3,256,512]{2,3,1,0:T(8,128)(2,1)}) %all-reduce.2.cloned.1.call-update) | async-done | bytes 2359312 | tf_op jit(solution)/shard_map/psum | solution.py:9
  158.0 0.0 copy-done
  158.0 7.9 %convolution_bitcast_fusion = f32[256,3,6,512]{0,3,2,1:T(8,128)} fusion(bf16[3,3,256,512]{2,3,1,0:T(8,128)(2,1)} %all-reduce.2.cloned.1.call-done, bf16[6,256,3,256]{3,1,2,0:T(8,128)(2,1)S(1)} %copy-done), kind=kOutput, calls=%fused_computation | convolution fusion | flops 3623878656 | bytes 14155776 | tf_op jit(solution)/shard_map/aibj,sbjw->isaw/dot_general | solution.py:13
  166.0 11.9 %copy.30 = f32[256,3,6,512]{3,2,1,0:T(8,128)} copy(f32[256,3,6,512]{0,3,2,1:T(8,128)} %convolution_bitcast_fusion) | data formatting | bytes 18874368 | tf_op jit(solution)/shard_map/aibj,sbjw->isaw/transpose | solution.py:13
  177.8 0.0 reduce-scatter.3.cloned.1.call-update
  177.8 0.0 reduce-scatter.5.cloned.1.call-start
  177.9 129.2 %reduce-scatter.3.cloned.1.call-done = f32[32,3,6,512]{3,2,1,0:T(8,128)} async-done(((f32[256,3,6,512]{3,2,1,0:T(8,128)}), f32[32,3,6,512]{3,2,1,0:T(8,128)}) %reduce-scatter.3.cloned.1.call-update) | async-done | bytes 1179664 | tf_op jit(solution)/shard_map/reduce_scatter | solution.py:43
  307.1 1.8 fusion.13
  308.9 3.4 convolution_bitcast_fusion.1
  312.3 0.0 copy-start.2
  312.3 0.0 reduce-scatter.5.cloned.1.call-update
  312.3 1.0 copy.32
  313.3 138.8 %reduce-scatter.5.cloned.1.call-done = f32[3,16,512]{2,1,0:T(8,128)} async-done(((f32[3,512,512]{2,1,0:T(8,128)}), f32[3,16,512]{2,1,0:T(8,128)}) %reduce-scatter.5.cloned.1.call-update) | async-done | bytes 98320 | tf_op jit(solution)/shard_map/reduce_scatter | solution.py:51
  452.1 0.0 copy-done.2
  452.1 1.5 sub.3
  (3 shorter events, 0.1 us)
Async XLA Ops:
  7.2 150.9 %copy-start = (bf16[6,256,3,256]{3,1,2,0:T(8,128)(2,1)S(1)}, bf16[6,256,3,256]{3,1,2,0:T(8,128)(2,1)}, u32[]{:S(2)}) copy-start(bf16[6,256,3,256]{3,1,2,0:T(8,128)(2,1)} %param.4) | copy-start | bytes 7077892
  9.4 0.8 copy-start.1
  16.6 61.1 %all-to-all-start = ((bf16[8,3,3,1,32,512]{5,4,2,1,3,0:T(8,128)(2,1)}), bf16[8,3,3,1,32,512]{5,4,2,1,3,0:T(8,128)(2,1)}, u32[]{:S(2)}, u32[]{:S(2)}) async-start(bf16[8,3,3,1,32,512]{5,4,2,1,3,0:T(8,128)(2,1)} %fusion.4), calls=%async_computation | async-start | bytes 4718592 | tf_op jit(solution)/shard_map/all_to_all | solution.py:39
  22.9 135.1 %all-reduce.2.cloned.1.call-start = ((), (), s32[]{:S(2)}) async-start(), calls=%async_computation.3 | async-start | bytes 4718592 | tf_op jit(solution)/shard_map/psum | solution.py:9
  85.4 221.7 %reduce-scatter.3.cloned.1.call-start = ((), (), s32[]{:S(2)}) async-start(), calls=%async_computation.4 | async-start | bytes 14155776 | tf_op jit(solution)/shard_map/reduce_scatter | solution.py:43
  177.8 274.2 %reduce-scatter.5.cloned.1.call-start = ((), (), s32[]{:S(2)}) async-start(), calls=%async_computation.5 | async-start | bytes 3244032 | tf_op jit(solution)/shard_map/reduce_scatter | solution.py:51
  312.3 139.8 %copy-start.2 = (f32[3,16,512]{2,1,0:T(8,128)S(1)}, f32[3,16,512]{2,1,0:T(8,128)}, u32[]{:S(2)}) copy-start(f32[3,16,512]{2,1,0:T(8,128)} %param.7) | copy-start | bytes 294916
Sparse Core Ops, SparseCore 0:
  85.5 72.4 all-reduce.1
  178.0 129.1 reduce-scatter.2
  312.4 139.6 reduce-scatter.4
